TPU v7x, 32 devices: a whole 2x2x4 slice. The times are simulated.
32 devices in a mesh: section: 2 (over y), design: 8 (over z, x), batch: 2 (over core).
Axes of the slice: x: 2, y: 2, z: 4, core: 2. Of those that a mesh axis runs over, the one named last changes fastest.
Arguments:
- samples: float32 [64, 4096], replicated, may hold values from -6 to 6
- order: int32 [4096], P('batch'), may hold values from 0 to 4095, each once
- design_points: bfloat16 [2, 64, 16384], P('section', None, 'design'), may hold values from -6 to 6
- weights: bfloat16 [2, 64, 16384], P('section', None, 'design'), may hold values from -2 to 2
- length_sq: float32 [2, 64], replicated, may hold values from 8 to 128
Outputs:
- moments: float32 [2, 4, 64, 1024], P('section', None, None, ('batch', 'design'))
Inputs may be any that keep to these rules, and one draw needn't show every extreme that they name: `order`: each sample index appears exactly once.
All inputs are finite; a program needn't handle non-finite values.
Results may differ from a plain program's by a relative error of at most 0.0037.
Values may be sent and summed in bfloat16 or wider, within the bound.
A program may use at most 64 MiB of HBM per device.

v0:
```python
import jax
import jax.numpy as jnp
from jax import lax
from jax.sharding import PartitionSpec as P

MICRO = 512


def passed_along(block, axis, distance):
    devices = range(lax.axis_size(axis))
    route = [(i - distance, i) for i in devices if i - distance in devices]
    return lax.ppermute(block, axis, route)


def local_sum(mean_in, var_in, points, squares, weight_rows, lengths):
    denom = lengths[:, None] + 2.0 * var_in
    offset = jnp.sum(mean_in * mean_in / denom, axis=0)
    log_scale = -0.5 * jnp.sum(jnp.log(1.0 + 2.0 * var_in / lengths[:, None]), axis=0)
    scaled = (mean_in / denom).astype(jnp.bfloat16)
    inverse = (1.0 / denom).astype(jnp.bfloat16)
    cross = lax.dot_general(
        scaled, points, (((0,), (0,)), ((), ())), preferred_element_type=jnp.float32
    )
    quad = lax.dot_general(
        inverse, squares, (((0,), (0,)), ((), ())), preferred_element_type=jnp.float32
    )
    kernel = jnp.exp(log_scale[:, None] - offset[:, None] + 2.0 * cross - quad).astype(jnp.bfloat16)
    return lax.dot_general(
        weight_rows, kernel, (((1,), (1,)), ((), ())), preferred_element_type=jnp.float32
    )


def square_of(points):
    wide = points.astype(jnp.float32)
    return (wide * wide).astype(jnp.bfloat16)


def shards(samples, order, design_points, weights, length_sq):
    section_index = lax.axis_index("section")
    is_first = section_index == 0
    points = design_points[0]
    weight_rows = weights[0]
    lengths = jnp.where(is_first, length_sq[0], length_sq[1])
    squares = square_of(points)
    feat = points.shape[0]
    half = feat // 2
    count = order.shape[0] // MICRO
    share = MICRO // lax.axis_size("design")
    column = lax.axis_index("design") * share

    def pick(turn):
        indices = order[turn * MICRO : (turn + 1) * MICRO]
        return jnp.take(samples, indices, axis=1)

    received = jnp.zeros((feat, MICRO), jnp.float32)
    zeros_rest = jnp.zeros((feat - half, MICRO), jnp.float32)
    firsts = []
    seconds = []
    for turn in range(count + 1):
        current = pick(min(turn, count - 1))
        earlier = pick(max(turn - 1, 0))
        moments_in = received
        later_mean = jnp.concatenate([moments_in[:half], earlier[half:]], axis=0)
        later_var = jnp.concatenate([moments_in[half:], zeros_rest], axis=0)
        mean_in = jnp.where(is_first, current, later_mean)
        var_in = jnp.where(is_first, 0.0, later_var)
        partial_sum = local_sum(mean_in, var_in, points, squares, weight_rows, lengths)
        summed = lax.psum(partial_sum, "design")
        layer_out = jnp.where(
            is_first,
            jnp.concatenate([summed[:half], jax.nn.softplus(summed[half:])], axis=0),
            summed,
        )
        received = passed_along(layer_out, "section", 1)
        block = lax.dynamic_slice_in_dim(layer_out, column, share, 1)
        if turn < count:
            firsts.append(block)
        if turn > 0:
            seconds.append(block)
    result = jnp.where(is_first, jnp.stack(firsts, axis=0), jnp.stack(seconds, axis=0))
    return result[None]


def solution(mesh):
    placed = (P(), P("batch"), P("section", None, "design"), P("section", None, "design"), P())
    return jax.shard_map(
        shards,
        mesh=mesh,
        in_specs=placed,
        out_specs=P("section", None, None, ("batch", "design")),
        check_vma=False,
    )
```

profile of v0, /device:TPU:0, one launch (start us, length us, event | category | flops | bytes accessed | tf_op | source)
XLA Modules:
  0.0 447.8 jit_solution(6106497824247773900)
XLA Ops:
  6.5 0.0 copy-start
  6.5 0.8 compare_and_fusion
  7.3 0.8 compare_select_fusion.5
  8.1 0.8 divide_convert_fusion.22
  8.9 0.6 log_reduce_fusion.4
  9.5 1.8 copy.6
  11.3 1.0 gather_fusion
  12.4 0.1 copy.7
  12.5 0.1 fusion.29
  12.6 2.7 fusion.23
  16.1 4.4 fusion.9
  20.5 0.0 all-reduce.11.cloned.1.call-update
  20.5 0.0 all-reduce.13.cloned.1.call-start
  20.5 73.3 %all-reduce.11.cloned.1.call-done = f32[64,512]{1,0:T(8,128)} async-done(((f32[64,512]{1,0:T(8,128)}), f32[64,512]{1,0:T(8,128)}) %all-reduce.11.cloned.1.call-update) | async-done | bytes 131088 | tf_op jit(solution)/shard_map/psum | solution.py:68
  93.8 0.9 fusion.144
  94.8 4.3 collective-permute-start
  99.1 1.0 gather_fusion.1
  100.1 0.1 copy.9
  100.3 1.3 collective-permute-done
  101.6 0.1 log_reduce_fusion.3
  101.7 2.7 fusion.21
  104.5 4.4 fusion.8
  108.9 0.0 all-reduce.13.cloned.1.call-update
  108.9 0.0 all-reduce.15.cloned.1.call-start
  109.0 70.6 %all-reduce.13.cloned.1.call-done = f32[64,512]{1,0:T(8,128)} async-done(((f32[64,512]{1,0:T(8,128)}), f32[64,512]{1,0:T(8,128)}) %all-reduce.13.cloned.1.call-update) | async-done | bytes 131088 | tf_op jit(solution)/shard_map/psum | solution.py:68
  179.6 0.9 fusion.142
  180.6 4.9 %collective-permute-start.1 = (f32[64,512]{1,0:T(8,128)S(1)}, f32[64,512]{1,0:T(8,128)}, u32[]{:S(2)}, u32[]{:S(2)}) collective-permute-start(f32[64,512]{1,0:T(8,128)S(1)} %maximum_select_fusion.2), channel_id=1, source_target_pairs={{0,16},{1,17},{2,18},{3,19},{4,20},{5,21},{6,22},{7,23},{8,24},{9,... | collective-permute-start | bytes 393224 | tf_op jit(solution)/shard_map/ppermute | solution.py:12
  185.5 1.0 gather_fusion.2
  186.5 0.1 copy.11
  186.7 0.7 collective-permute-done.1
  187.3 0.9 fusion.141
  188.2 0.1 log_reduce_fusion.2
  188.4 2.7 fusion.19
  191.1 4.4 fusion.7
  195.5 0.0 all-reduce.15.cloned.1.call-update
  195.5 0.0 all-reduce.17.cloned.1.call-start
  195.6 70.7 %all-reduce.15.cloned.1.call-done = f32[64,512]{1,0:T(8,128)} async-done(((f32[64,512]{1,0:T(8,128)}), f32[64,512]{1,0:T(8,128)}) %all-reduce.15.cloned.1.call-update) | async-done | bytes 131088 | tf_op jit(solution)/shard_map/psum | solution.py:68
  266.3 0.9 fusion.140
  267.3 4.9 %collective-permute-start.2 = (f32[64,512]{1,0:T(8,128)S(1)}, f32[64,512]{1,0:T(8,128)}, u32[]{:S(2)}, u32[]{:S(2)}) collective-permute-start(f32[64,512]{1,0:T(8,128)S(1)} %maximum_select_fusion.4), channel_id=1, source_target_pairs={{0,16},{1,17},{2,18},{3,19},{4,20},{5,21},{6,22},{7,23},{8,24},{9,... | collective-permute-start | bytes 393224 | tf_op jit(solution)/shard_map/ppermute | solution.py:12
  272.2 1.0 gather_fusion.3
  273.2 0.1 copy.13
  273.4 0.7 collective-permute-done.2
  274.1 0.9 fusion.139
  275.0 0.1 log_reduce_fusion.1
  275.1 2.7 fusion.17
  277.8 4.4 fusion.6
  282.2 0.0 all-reduce.17.cloned.1.call-update
  282.3 0.0 all-reduce.19.cloned.1.call-start
  282.3 70.8 %all-reduce.17.cloned.1.call-done = f32[64,512]{1,0:T(8,128)} async-done(((f32[64,512]{1,0:T(8,128)}), f32[64,512]{1,0:T(8,128)}) %all-reduce.17.cloned.1.call-update) | async-done | bytes 131088 | tf_op jit(solution)/shard_map/psum | solution.py:68
  353.1 0.9 fusion.138
  354.0 4.3 collective-permute-start.3
  358.3 0.1 dynamic-slice_bitcast_fusion.3
  358.4 0.1 dynamic-slice_bitcast_fusion.2
  358.5 2.3 collective-permute-done.3
  360.8 0.1 log_reduce_fusion
  361.0 2.7 fusion.15
  363.7 4.4 fusion.5
  368.1 0.0 all-reduce.19.cloned.1.call-update
  368.1 0.1 dynamic-slice_bitcast_fusion.1
  368.2 0.1 dynamic-slice_bitcast_fusion
  368.3 70.5 %all-reduce.19.cloned.1.call-done = f32[64,512]{1,0:T(8,128)} async-done(((f32[64,512]{1,0:T(8,128)}), f32[64,512]{1,0:T(8,128)}) %all-reduce.19.cloned.1.call-update) | async-done | bytes 131088 | tf_op jit(solution)/shard_map/psum | solution.py:68
  438.8 0.9 compare_select_fusion
  439.8 0.8 fusion.94
  440.6 0.7 maximum_select_fusion.7
  (22 shorter events, 0.2 us)
Async XLA Ops:
  6.5 9.5 %copy-start = (bf16[1,64,2048]{2,1,0:T(8,128)(2,1)S(1)}, bf16[1,64,2048]{2,1,0:T(8,128)(2,1)}, u32[]{:S(2)}) copy-start(bf16[1,64,2048]{2,1,0:T(8,128)(2,1)} %param.10) | copy-start | bytes 786436
  6.5 6.1 %copy-start.1 = (bf16[1,64,2048]{2,1,0:T(8,128)(2,1)S(1)}, bf16[1,64,2048]{2,1,0:T(8,128)(2,1)}, u32[]{:S(2)}) copy-start(bf16[1,64,2048]{2,1,0:T(8,128)(2,1)} %param.9) | copy-start | bytes 786436
  6.5 87.3 %all-reduce.11.cloned.1.call-start = ((), (), s32[]{:S(2)}) async-start(), calls=%async_computation | async-start | bytes 262144 | tf_op jit(solution)/shard_map/psum | solution.py:68
  20.5 159.1 %all-reduce.13.cloned.1.call-start = ((), (), s32[]{:S(2)}) async-start(), calls=%async_computation.1 | async-start | bytes 262144 | tf_op jit(solution)/shard_map/psum | solution.py:68
  94.8 6.8 %collective-permute-start = (f32[64,512]{1,0:T(8,128)S(1)}, f32[64,512]{1,0:T(8,128)S(1)}, u32[]{:S(2)}, u32[]{:S(2)}) collective-permute-start(f32[64,512]{1,0:T(8,128)S(1)} %maximum_select_fusion), channel_id=1, source_target_pairs={{0,16},{1,17},{2,18},{3,19},{4,20},{5,21},{6,22},{7,23},{8,24},{9,... | collective-permute-start | bytes 393224 | tf_op jit(solution)/shard_map/ppermute | solution.py:12
  108.9 157.4 %all-reduce.15.cloned.1.call-start = ((), (), s32[]{:S(2)}) async-start(), calls=%async_computation.2 | async-start | bytes 262144 | tf_op jit(solution)/shard_map/psum | solution.py:68
  180.6 6.8 %collective-permute-start.1 = (f32[64,512]{1,0:T(8,128)S(1)}, f32[64,512]{1,0:T(8,128)}, u32[]{:S(2)}, u32[]{:S(2)}) collective-permute-start(f32[64,512]{1,0:T(8,128)S(1)} %maximum_select_fusion.2), channel_id=1, source_target_pairs={{0,16},{1,17},{2,18},{3,19},{4,20},{5,21},{6,22},{7,23},{8,24},{9,... | collective-permute-start | bytes 393224 | tf_op jit(solution)/shard_map/ppermute | solution.py:12
  195.5 157.5 %all-reduce.17.cloned.1.call-start = ((), (), s32[]{:S(2)}) async-start(), calls=%async_computation.3 | async-start | bytes 262144 | tf_op jit(solution)/shard_map/psum | solution.py:68
  267.3 6.8 %collective-permute-start.2 = (f32[64,512]{1,0:T(8,128)S(1)}, f32[64,512]{1,0:T(8,128)}, u32[]{:S(2)}, u32[]{:S(2)}) collective-permute-start(f32[64,512]{1,0:T(8,128)S(1)} %maximum_select_fusion.4), channel_id=1, source_target_pairs={{0,16},{1,17},{2,18},{3,19},{4,20},{5,21},{6,22},{7,23},{8,24},{9,... | collective-permute-start | bytes 393224 | tf_op jit(solution)/shard_map/ppermute | solution.py:12
  282.3 156.6 %all-reduce.19.cloned.1.call-start = ((), (), s32[]{:S(2)}) async-start(), calls=%async_computation.4 | async-start | bytes 262144 | tf_op jit(solution)/shard_map/psum | solution.py:68
  354.0 6.8 %collective-permute-start.3 = (f32[64,512]{1,0:T(8,128)S(1)}, f32[64,512]{1,0:T(8,128)S(1)}, u32[]{:S(2)}, u32[]{:S(2)}) collective-permute-start(f32[64,512]{1,0:T(8,128)S(1)} %maximum_select_fusion.6), channel_id=1, source_target_pairs={{0,16},{1,17},{2,18},{3,19},{4,20},{5,21},{6,22},{7,23},{8,24},{9,... | collective-permute-start | bytes 393224 | tf_op jit(solution)/shard_map/ppermute | solution.py:12
Sparse Core Ops, SparseCore 0:
  20.6 73.1 all-reduce.10
  109.0 70.5 all-reduce.12
  195.7 70.6 all-reduce.14
  282.4 70.6 all-reduce.16
  368.3 70.5 all-reduce.18
where the time goes:
time: 449 us; the launch traced here: 448 us
  waiting for transfers between devices  361 us (80%)
  matrix products  35.7 us (8%)
  starting transfers between devices  18.6 us (4%)
  between operations  14 us (3%)
  other arithmetic  9.83 us (2%)
  local copies, waits for them, and re-layouts  8.53 us (2%)
    psum x5, waiting for transfers between devices, shards(): summed = lax.psum(partial_sum, 'design')  356 us
    dot_general x5, matrix products, local_sum(): lax.dot_general(weight_rows, kernel, (((1,), (1,)), ((), ())), preferred_...  22.1 us
    ppermute x4, starting transfers between devices, passed_along(): return lax.ppermute(block, axis, route)  18.4 us
    dot_general x5, matrix products, local_sum(): lax.dot_general(scaled, points, (((0,), (0,)), ((), ())), preferred_eleme...  13.6 us
  transfers between devices with their start and end apart: 9, of which 9 were waited for; matrix products, arithmetic and copies ran while one was open for 1% of the time, Pallas kernels for 0%

commit v1 on v0

--- a/solution.py
+++ b/solution.py
@@ -4,6 +4,16 @@
 from jax.sharding import PartitionSpec as P
 
 MICRO = 512
+
+
+def _store_pieces_all(block_here):
+    num = lax.axis_size("design")
+    clean = block_here
+    for t in [hop_no for hop_no in (1, 2, 4, 8, 16) if hop_no < num]:
+        clean = clean + lax.ppermute(
+            clean, axis_name="design", perm=[(kk, kk ^ t) for kk in range(num)]
+        )
+    return clean
 
 
 def passed_along(block, axis, distance):
@@ -65,7 +75,7 @@
         mean_in = jnp.where(is_first, current, later_mean)
         var_in = jnp.where(is_first, 0.0, later_var)
         partial_sum = local_sum(mean_in, var_in, points, squares, weight_rows, lengths)
-        summed = lax.psum(partial_sum, "design")
+        summed = _store_pieces_all(partial_sum)
         layer_out = jnp.where(
             is_first,
             jnp.concatenate([summed[:half], jax.nn.softplus(summed[half:])], axis=0),

time: 449 us -> 159 us (0.35)
  waiting for transfers between devices: 361 us -> 71.6 us
  starting transfers between devices: 18.6 us -> 39.3 us
  between operations: 14 us -> 1 us
  other arithmetic: 9.83 us -> 4.97 us
    psum x5 -> x0, waiting for transfers between devices: 356 us -> none  [shards(): summed = lax.psum(partial_sum, 'design')]
    ppermute x0 -> x15, waiting for transfers between devices: none -> 66.6 us  [_store_pieces_all(): lax.ppermute(clean, axis_name='design', perm=[(kk, kk ^ t) for kk in rang...]
    ppermute x0 -> x15, starting transfers between devices: none -> 20.9 us  [_store_pieces_all(): lax.ppermute(clean, axis_name='design', perm=[(kk, kk ^ t) for kk in rang...]
  transfers between devices with their start and end apart: 9 -> 19, of which waited for: 9 -> 19; matrix products, arithmetic and copies ran while one was open for 1% -> 2% of each run, Pallas kernels for 0% -> 0%
where the time goes in v1:
time: 159 us; the launch traced here: 158 us
  waiting for transfers between devices  71.6 us (45%)
  starting transfers between devices  39.3 us (25%)
  matrix products  32.5 us (20%)
  local copies, waits for them, and re-layouts  8.53 us (5%)
  other arithmetic  4.97 us (3%)
    ppermute x15, waiting for transfers between devices, _store_pieces_all(): lax.ppermute(clean, axis_name='design', perm=[(kk, kk ^ t) for kk in rang...  66.6 us
    ppermute x15, starting transfers between devices, _store_pieces_all(): lax.ppermute(clean, axis_name='design', perm=[(kk, kk ^ t) for kk in rang...  20.9 us
    dot_general x5, matrix products, local_sum(): lax.dot_general(weight_rows, kernel, (((1,), (1,)), ((), ())), preferred_...  18.8 us
    ppermute x4, starting transfers between devices, passed_along(): return lax.ppermute(block, axis, route)  18.4 us
    dot_general x5, matrix products, local_sum(): lax.dot_general(scaled, points, (((0,), (0,)), ((), ())), preferred_eleme...  13.8 us
    ppermute x4, waiting for transfers between devices, passed_along(): return lax.ppermute(block, axis, route)  5 us
    gather x8, local copies, waits for them, and re-layouts, pick(): return jnp.take(samples, indices, axis=1)  4.58 us
  transfers between devices with their start and end apart: 19, of which 19 were waited for; matrix products, arithmetic and copies ran while one was open for 2% of the time, Pallas kernels for 0%

profile of v1, /device:TPU:0, one launch (start us, length us, event | category | flops | bytes accessed | tf_op | source)
XLA Modules:
  0.0 157.9 jit_solution(5990265104182746584)
XLA Ops:
  0.0 0.8 compare_and_fusion
  0.8 0.8 compare_select_fusion.5
  1.6 0.8 divide_convert_fusion.22
  2.3 0.6 log_reduce_fusion.4
  3.0 1.8 %copy.6 = f32[64,4096]{0,1:T(8,128)S(1)} copy(f32[64,4096]{1,0:T(8,128)} %param.7) | data formatting | bytes 2097152 | tf_op args[0]
  4.8 1.0 gather_fusion
  5.9 0.1 copy.7
  6.1 2.8 %fusion.23 = f32[512,2048]{1,0:T(8,128)} fusion(bf16[1,64,2048]{2,1,0:T(8,128)(2,1)S(1)} %copy-done.1, f32[64,512]{1,0:T(8,128)S(1)} %select_bitcast_fusion.3, f32[32,512]{1,0:T(8,128)S(1)} %slice.127, f32[64]{0:T(128)S(1)} %get-tuple-element.18, pred[]{:T(512)S(6)} %eq.3), kind=kOutput, calls=%fused_computation.33 | convolution fusion | flops 134316032 | bytes 4653313 | tf_op jit(solution)/shard_map/dot_general | solution.py:31
  9.5 3.7 %fusion.9 = f32[64,512]{1,0:T(8,128)S(1)} fusion(f32[512,2048]{1,0:T(8,128)} %fusion.23, f32[512]{0:T(512)S(1)} %broadcast_subtract_fusion, bf16[1,64,2048]{2,1,0:T(8,128)(2,1)S(1)} %copy-done, bf16[1,64,2048]{2,1,0:T(8,128)(2,1)S(1)} %copy-done.1, bf16[64]{0:T(256)(128)(2,1)S(1)} %get-tuple-element.17), kind=kOutput, calls=%fused_computation.18 | convolution fusion | flops 273022976 | bytes 4851840 | tf_op jit(solution)/shard_map/dot_general | solution.py:38
  13.3 3.0 %collective-permute-start = (f32[64,512]{1,0:T(8,128)S(1)}, f32[64,512]{1,0:T(8,128)S(1)}, u32[]{:S(2)}, u32[]{:S(2)}) collective-permute-start(f32[64,512]{1,0:T(8,128)S(1)} %fusion.9), channel_id=1, source_target_pairs={{0,2},{2,0},{4,6},{6,4},{8,10},{10,8},{12,14},{14,12},{1,3},{3,1},... | collective-permute-start | bytes 393224 | tf_op jit(solution)/shard_map/ppermute | solution.py:13
  16.3 3.5 %collective-permute-done = f32[64,512]{1,0:T(8,128)S(1)} collective-permute-done((f32[64,512]{1,0:T(8,128)S(1)}, f32[64,512]{1,0:T(8,128)S(1)}, u32[]{:S(2)}, u32[]{:S(2)}) %collective-permute-start) | collective-permute-done | bytes 131104 | tf_op jit(solution)/shard_map/ppermute | solution.py:13
  19.8 1.9 %collective-permute-start.1 = (f32[64,512]{1,0:T(8,128)S(1)}, f32[64,512]{1,0:T(8,128)S(1)}, u32[]{:S(2)}, u32[]{:S(2)}) collective-permute-start(f32[64,512]{1,0:T(8,128)S(1)} %add.172), channel_id=1, source_target_pairs={{0,4},{2,6},{4,0},{6,2},{8,12},{10,14},{12,8},{14,10},{1,5},{3,7},... | collective-permute-start | bytes 393224 | tf_op jit(solution)/shard_map/ppermute | solution.py:13
  21.7 3.1 %collective-permute-done.1 = f32[64,512]{1,0:T(8,128)S(1)} collective-permute-done((f32[64,512]{1,0:T(8,128)S(1)}, f32[64,512]{1,0:T(8,128)S(1)}, u32[]{:S(2)}, u32[]{:S(2)}) %collective-permute-start.1) | collective-permute-done | bytes 131104 | tf_op jit(solution)/shard_map/ppermute | solution.py:13
  24.9 2.9 %collective-permute-start.2 = (f32[64,512]{1,0:T(8,128)S(1)}, f32[64,512]{1,0:T(8,128)S(1)}, u32[]{:S(2)}, u32[]{:S(2)}) collective-permute-start(f32[64,512]{1,0:T(8,128)S(1)} %add.173), channel_id=1, source_target_pairs={{0,8},{2,10},{4,12},{6,14},{8,0},{10,2},{12,4},{14,6},{1,9},{3,11}... | collective-permute-start | bytes 393224 | tf_op jit(solution)/shard_map/ppermute | solution.py:13
  27.8 4.4 %collective-permute-done.2 = f32[64,512]{1,0:T(8,128)S(1)} collective-permute-done((f32[64,512]{1,0:T(8,128)S(1)}, f32[64,512]{1,0:T(8,128)S(1)}, u32[]{:S(2)}, u32[]{:S(2)}) %collective-permute-start.2) | collective-permute-done | bytes 131104 | tf_op jit(solution)/shard_map/ppermute | solution.py:13
  32.3 3.7 %collective-permute-start.3 = (f32[64,512]{1,0:T(8,128)S(1)}, f32[64,512]{1,0:T(8,128)S(1)}, u32[]{:S(2)}, u32[]{:S(2)}) collective-permute-start(f32[64,512]{1,0:T(8,128)S(1)} %maximum_select_fusion), channel_id=1, source_target_pairs={{0,16},{1,17},{2,18},{3,19},{4,20},{5,21},{6,22},{7,23},{8,24},{9,... | collective-permute-start | bytes 393224 | tf_op jit(solution)/shard_map/ppermute | solution.py:22
  36.0 1.0 gather_fusion.1
  37.1 0.1 copy.9
  37.2 1.3 collective-permute-done.3
  38.5 0.1 log_reduce_fusion.3
  38.7 2.8 %fusion.21 = f32[512,2048]{1,0:T(8,128)} fusion(bf16[1,64,2048]{2,1,0:T(8,128)(2,1)S(1)} %copy-done.1, f32[32,512]{1,0:T(8,128)S(1)} %get-tuple-element.34, f32[64]{0:T(128)S(1)} %get-tuple-element.18, pred[]{:T(512)S(6)} %eq.3, f32[64,512]{1,0:T(8,128)S(1)} %get-tuple-element.16, f32[32,512]{1,0:T(8,128)S(1)} %slice.127, f32[32,512]{1,0:T(8,128)S(1)} %get-tuple-element.33), kind=kOutput, calls=%fused_computation.31 | convolution fusion | flops 134447104 | bytes 4784385 | tf_op jit(solution)/shard_map/dot_general | solution.py:31
  41.4 3.8 %fusion.8 = f32[64,512]{1,0:T(8,128)S(1)} fusion(f32[512,2048]{1,0:T(8,128)} %fusion.21, f32[512]{0:T(512)S(1)} %multiply_subtract_fusion.3, bf16[1,64,2048]{2,1,0:T(8,128)(2,1)S(1)} %copy-done, bf16[1,64,2048]{2,1,0:T(8,128)(2,1)S(1)} %copy-done.1, f32[32,512]{1,0:T(8,128)S(1)} %get-tuple-element.34, f32[64]{0:T(128)S(1)} %get-tuple-element.18, pred[]{:T(512)S(6)} %eq.3), kind=kOutput, calls=%fused_computation.17 | convolution fusion | flops 273186816 | bytes 4917505 | tf_op jit(solution)/shard_map/dot_general | solution.py:38
  45.2 1.6 collective-permute-start.4
  46.7 3.5 %collective-permute-done.4 = f32[64,512]{1,0:T(8,128)S(1)} collective-permute-done((f32[64,512]{1,0:T(8,128)S(1)}, f32[64,512]{1,0:T(8,128)S(1)}, u32[]{:S(2)}, u32[]{:S(2)}) %collective-permute-start.4) | collective-permute-done | bytes 131104 | tf_op jit(solution)/shard_map/ppermute | solution.py:13
  50.2 0.7 collective-permute-start.5
  51.0 4.7 %collective-permute-done.5 = f32[64,512]{1,0:T(8,128)S(1)} collective-permute-done((f32[64,512]{1,0:T(8,128)S(1)}, f32[64,512]{1,0:T(8,128)S(1)}, u32[]{:S(2)}, u32[]{:S(2)}) %collective-permute-start.5) | collective-permute-done | bytes 131104 | tf_op jit(solution)/shard_map/ppermute | solution.py:13
  55.7 2.1 %collective-permute-start.6 = (f32[64,512]{1,0:T(8,128)S(1)}, f32[64,512]{1,0:T(8,128)S(1)}, u32[]{:S(2)}, u32[]{:S(2)}) collective-permute-start(f32[64,512]{1,0:T(8,128)S(1)} %add.182), channel_id=1, source_target_pairs={{0,8},{2,10},{4,12},{6,14},{8,0},{10,2},{12,4},{14,6},{1,9},{3,11}... | collective-permute-start | bytes 393224 | tf_op jit(solution)/shard_map/ppermute | solution.py:13
  57.8 5.2 %collective-permute-done.6 = f32[64,512]{1,0:T(8,128)S(1)} collective-permute-done((f32[64,512]{1,0:T(8,128)S(1)}, f32[64,512]{1,0:T(8,128)S(1)}, u32[]{:S(2)}, u32[]{:S(2)}) %collective-permute-start.6) | collective-permute-done | bytes 131104 | tf_op jit(solution)/shard_map/ppermute | solution.py:13
  63.2 5.0 %collective-permute-start.7 = (f32[64,512]{1,0:T(8,128)S(1)}, f32[64,512]{1,0:T(8,128)}, u32[]{:S(2)}, u32[]{:S(2)}) collective-permute-start(f32[64,512]{1,0:T(8,128)S(1)} %maximum_select_fusion.2), channel_id=1, source_target_pairs={{0,16},{1,17},{2,18},{3,19},{4,20},{5,21},{6,22},{7,23},{8,24},{9,... | collective-permute-start | bytes 393224 | tf_op jit(solution)/shard_map/ppermute | solution.py:22
  68.2 1.0 gather_fusion.2
  69.3 0.7 collective-permute-done.7
  70.0 0.9 fusion.141
  70.9 0.1 log_reduce_fusion.2
  71.0 2.8 %fusion.19 = f32[512,2048]{1,0:T(8,128)} fusion(bf16[1,64,2048]{2,1,0:T(8,128)(2,1)S(1)} %copy-done.1, f32[32,512]{1,0:T(8,128)S(1)} %get-tuple-element.30, f32[64]{0:T(128)S(1)} %get-tuple-element.18, pred[]{:T(512)S(6)} %eq.3, f32[64,512]{1,0:T(8,128)S(1)} %get-tuple-element.15, f32[32,512]{1,0:T(8,128)S(1)} %slice.136, f32[32,512]{1,0:T(8,128)S(1)} %get-tuple-element.29), kind=kOutput, calls=%fused_computation.29 | convolution fusion | flops 134447104 | bytes 4784385 | tf_op jit(solution)/shard_map/dot_general | solution.py:31
  73.8 3.8 %fusion.7 = f32[64,512]{1,0:T(8,128)S(1)} fusion(f32[512,2048]{1,0:T(8,128)} %fusion.19, f32[512]{0:T(512)S(1)} %multiply_subtract_fusion.2, bf16[1,64,2048]{2,1,0:T(8,128)(2,1)S(1)} %copy-done, bf16[1,64,2048]{2,1,0:T(8,128)(2,1)S(1)} %copy-done.1, f32[32,512]{1,0:T(8,128)S(1)} %get-tuple-element.30, f32[64]{0:T(128)S(1)} %get-tuple-element.18, pred[]{:T(512)S(6)} %eq.3), kind=kOutput, calls=%fused_computation.16 | convolution fusion | flops 273186816 | bytes 4917505 | tf_op jit(solution)/shard_map/dot_general | solution.py:38
  77.5 1.6 %collective-permute-start.8 = (f32[64,512]{1,0:T(8,128)S(1)}, f32[64,512]{1,0:T(8,128)S(1)}, u32[]{:S(2)}, u32[]{:S(2)}) collective-permute-start(f32[64,512]{1,0:T(8,128)S(1)} %fusion.7), channel_id=1, source_target_pairs={{0,2},{2,0},{4,6},{6,4},{8,10},{10,8},{12,14},{14,12},{1,3},{3,1},... | collective-permute-start | bytes 393224 | tf_op jit(solution)/shard_map/ppermute | solution.py:13
  79.1 3.4 %collective-permute-done.8 = f32[64,512]{1,0:T(8,128)S(1)} collective-permute-done((f32[64,512]{1,0:T(8,128)S(1)}, f32[64,512]{1,0:T(8,128)S(1)}, u32[]{:S(2)}, u32[]{:S(2)}) %collective-permute-start.8) | collective-permute-done | bytes 131104 | tf_op jit(solution)/shard_map/ppermute | solution.py:13
  82.6 0.3 collective-permute-start.9
  82.9 4.7 %collective-permute-done.9 = f32[64,512]{1,0:T(8,128)S(1)} collective-permute-done((f32[64,512]{1,0:T(8,128)S(1)}, f32[64,512]{1,0:T(8,128)S(1)}, u32[]{:S(2)}, u32[]{:S(2)}) %collective-permute-start.9) | collective-permute-done | bytes 131104 | tf_op jit(solution)/shard_map/ppermute | solution.py:13
  87.7 1.5 collective-permute-start.10
  89.2 5.8 %collective-permute-done.10 = f32[64,512]{1,0:T(8,128)S(1)} collective-permute-done((f32[64,512]{1,0:T(8,128)S(1)}, f32[64,512]{1,0:T(8,128)S(1)}, u32[]{:S(2)}, u32[]{:S(2)}) %collective-permute-start.10) | collective-permute-done | bytes 131104 | tf_op jit(solution)/shard_map/ppermute | solution.py:13
  95.1 5.1 %collective-permute-start.11 = (f32[64,512]{1,0:T(8,128)S(1)}, f32[64,512]{1,0:T(8,128)}, u32[]{:S(2)}, u32[]{:S(2)}) collective-permute-start(f32[64,512]{1,0:T(8,128)S(1)} %maximum_select_fusion.4), channel_id=1, source_target_pairs={{0,16},{1,17},{2,18},{3,19},{4,20},{5,21},{6,22},{7,23},{8,24},{9,... | collective-permute-start | bytes 393224 | tf_op jit(solution)/shard_map/ppermute | solution.py:22
  100.2 1.0 gather_fusion.3
  101.4 0.7 collective-permute-done.11
  102.1 0.9 fusion.139
  102.9 0.1 log_reduce_fusion.1
  103.1 2.8 %fusion.17 = f32[512,2048]{1,0:T(8,128)} fusion(bf16[1,64,2048]{2,1,0:T(8,128)(2,1)S(1)} %copy-done.1, f32[32,512]{1,0:T(8,128)S(1)} %get-tuple-element.26, f32[64]{0:T(128)S(1)} %get-tuple-element.18, pred[]{:T(512)S(6)} %eq.3, f32[64,512]{1,0:T(8,128)S(1)} %get-tuple-element.14, f32[32,512]{1,0:T(8,128)S(1)} %slice.141, f32[32,512]{1,0:T(8,128)S(1)} %get-tuple-element.25), kind=kOutput, calls=%fused_computation.27 | convolution fusion | flops 134447104 | bytes 4784385 | tf_op jit(solution)/shard_map/dot_general | solution.py:31
  105.8 3.8 %fusion.6 = f32[64,512]{1,0:T(8,128)S(1)} fusion(f32[512,2048]{1,0:T(8,128)} %fusion.17, f32[512]{0:T(512)S(1)} %multiply_subtract_fusion.1, bf16[1,64,2048]{2,1,0:T(8,128)(2,1)S(1)} %copy-done, bf16[1,64,2048]{2,1,0:T(8,128)(2,1)S(1)} %copy-done.1, f32[32,512]{1,0:T(8,128)S(1)} %get-tuple-element.26, f32[64]{0:T(128)S(1)} %get-tuple-element.18, pred[]{:T(512)S(6)} %eq.3), kind=kOutput, calls=%fused_computation.15 | convolution fusion | flops 273186816 | bytes 4917505 | tf_op jit(solution)/shard_map/dot_general | solution.py:38
  109.6 1.6 collective-permute-start.12
  111.1 3.5 %collective-permute-done.12 = f32[64,512]{1,0:T(8,128)S(1)} collective-permute-done((f32[64,512]{1,0:T(8,128)S(1)}, f32[64,512]{1,0:T(8,128)S(1)}, u32[]{:S(2)}, u32[]{:S(2)}) %collective-permute-start.12) | collective-permute-done | bytes 131104 | tf_op jit(solution)/shard_map/ppermute | solution.py:13
  114.7 5.0 %collective-permute-done.13 = f32[64,512]{1,0:T(8,128)S(1)} collective-permute-done((f32[64,512]{1,0:T(8,128)S(1)}, f32[64,512]{1,0:T(8,128)S(1)}, u32[]{:S(2)}, u32[]{:S(2)}) %collective-permute-start.13) | collective-permute-done | bytes 131104 | tf_op jit(solution)/shard_map/ppermute | solution.py:13
  119.7 1.0 collective-permute-start.14
  120.7 5.8 %collective-permute-done.14 = f32[64,512]{1,0:T(8,128)S(1)} collective-permute-done((f32[64,512]{1,0:T(8,128)S(1)}, f32[64,512]{1,0:T(8,128)S(1)}, u32[]{:S(2)}, u32[]{:S(2)}) %collective-permute-start.14) | collective-permute-done | bytes 131104 | tf_op jit(solution)/shard_map/ppermute | solution.py:13
  126.6 4.6 %collective-permute-start.15 = (f32[64,512]{1,0:T(8,128)S(1)}, f32[64,512]{1,0:T(8,128)S(1)}, u32[]{:S(2)}, u32[]{:S(2)}) collective-permute-start(f32[64,512]{1,0:T(8,128)S(1)} %maximum_select_fusion.6), channel_id=1, source_target_pairs={{0,16},{1,17},{2,18},{3,19},{4,20},{5,21},{6,22},{7,23},{8,24},{9,... | collective-permute-start | bytes 393224 | tf_op jit(solution)/shard_map/ppermute | solution.py:22
  131.2 2.3 %collective-permute-done.15 = f32[64,512]{1,0:T(8,128)S(1)} collective-permute-done((f32[64,512]{1,0:T(8,128)S(1)}, f32[64,512]{1,0:T(8,128)S(1)}, u32[]{:S(2)}, u32[]{:S(2)}) %collective-permute-start.15) | collective-permute-done | bytes 131104 | tf_op jit(solution)/shard_map/ppermute | solution.py:22
  133.6 0.1 log_reduce_fusion
  133.7 2.8 %fusion.15 = f32[512,2048]{1,0:T(8,128)} fusion(bf16[1,64,2048]{2,1,0:T(8,128)(2,1)S(1)} %copy-done.1, f32[32,512]{1,0:T(8,128)S(1)} %get-tuple-element.22, f32[64]{0:T(128)S(1)} %get-tuple-element.18, pred[]{:T(512)S(6)} %eq.3, f32[64,512]{1,0:T(8,128)S(1)} %get-tuple-element.14, f32[32,512]{1,0:T(8,128)S(1)} %slice.146, f32[32,512]{1,0:T(8,128)S(1)} %get-tuple-element.21), kind=kOutput, calls=%fused_computation.25 | convolution fusion | flops 134447104 | bytes 4784385 | tf_op jit(solution)/shard_map/dot_general | solution.py:31
  136.4 3.8 %fusion.5 = f32[64,512]{1,0:T(8,128)S(1)} fusion(f32[512,2048]{1,0:T(8,128)} %fusion.15, f32[512]{0:T(512)S(1)} %multiply_subtract_fusion, bf16[1,64,2048]{2,1,0:T(8,128)(2,1)S(1)} %copy-done, bf16[1,64,2048]{2,1,0:T(8,128)(2,1)S(1)} %copy-done.1, f32[32,512]{1,0:T(8,128)S(1)} %get-tuple-element.22, f32[64]{0:T(128)S(1)} %get-tuple-element.18, pred[]{:T(512)S(6)} %eq.3), kind=kOutput, calls=%fused_computation.14 | convolution fusion | flops 273186816 | bytes 4917505 | tf_op jit(solution)/shard_map/dot_general | solution.py:38
  140.2 1.6 collective-permute-start.16
  141.8 3.5 %collective-permute-done.16 = f32[64,512]{1,0:T(8,128)S(1)} collective-permute-done((f32[64,512]{1,0:T(8,128)S(1)}, f32[64,512]{1,0:T(8,128)S(1)}, u32[]{:S(2)}, u32[]{:S(2)}) %collective-permute-start.16) | collective-permute-done | bytes 131104 | tf_op jit(solution)/shard_map/ppermute | solution.py:13
  145.5 4.8 %collective-permute-done.17 = f32[64,512]{1,0:T(8,128)S(1)} collective-permute-done((f32[64,512]{1,0:T(8,128)S(1)}, f32[64,512]{1,0:T(8,128)S(1)}, u32[]{:S(2)}, u32[]{:S(2)}) %collective-permute-start.17) | collective-permute-done | bytes 131104 | tf_op jit(solution)/shard_map/ppermute | solution.py:13
  150.3 1.0 collective-permute-start.18
  151.4 5.7 %collective-permute-done.18 = f32[64,512]{1,0:T(8,128)S(1)} collective-permute-done((f32[64,512]{1,0:T(8,128)S(1)}, f32[64,512]{1,0:T(8,128)S(1)}, u32[]{:S(2)}, u32[]{:S(2)}) %collective-permute-start.18) | collective-permute-done | bytes 131104 | tf_op jit(solution)/shard_map/ppermute | solution.py:13
  157.3 0.7 maximum_select_fusion.7
  (52 shorter events, 1.6 us)
Async XLA Ops:
  0.0 9.5 %copy-start = (bf16[1,64,2048]{2,1,0:T(8,128)(2,1)S(1)}, bf16[1,64,2048]{2,1,0:T(8,128)(2,1)}, u32[]{:S(2)}) copy-start(bf16[1,64,2048]{2,1,0:T(8,128)(2,1)} %param.10) | copy-start | bytes 786436
  0.0 6.1 %copy-start.1 = (bf16[1,64,2048]{2,1,0:T(8,128)(2,1)S(1)}, bf16[1,64,2048]{2,1,0:T(8,128)(2,1)}, u32[]{:S(2)}) copy-start(bf16[1,64,2048]{2,1,0:T(8,128)(2,1)} %param.9) | copy-start | bytes 786436
  13.3 6.5 %collective-permute-start = (f32[64,512]{1,0:T(8,128)S(1)}, f32[64,512]{1,0:T(8,128)S(1)}, u32[]{:S(2)}, u32[]{:S(2)}) collective-permute-start(f32[64,512]{1,0:T(8,128)S(1)} %fusion.9), channel_id=1, source_target_pairs={{0,2},{2,0},{4,6},{6,4},{8,10},{10,8},{12,14},{14,12},{1,3},{3,1},... | collective-permute-start | bytes 393224 | tf_op jit(solution)/shard_map/ppermute | solution.py:13
  19.8 5.0 %collective-permute-start.1 = (f32[64,512]{1,0:T(8,128)S(1)}, f32[64,512]{1,0:T(8,128)S(1)}, u32[]{:S(2)}, u32[]{:S(2)}) collective-permute-start(f32[64,512]{1,0:T(8,128)S(1)} %add.172), channel_id=1, source_target_pairs={{0,4},{2,6},{4,0},{6,2},{8,12},{10,14},{12,8},{14,10},{1,5},{3,7},... | collective-permute-start | bytes 393224 | tf_op jit(solution)/shard_map/ppermute | solution.py:13
  24.9 7.3 %collective-permute-start.2 = (f32[64,512]{1,0:T(8,128)S(1)}, f32[64,512]{1,0:T(8,128)S(1)}, u32[]{:S(2)}, u32[]{:S(2)}) collective-permute-start(f32[64,512]{1,0:T(8,128)S(1)} %add.173), channel_id=1, source_target_pairs={{0,8},{2,10},{4,12},{6,14},{8,0},{10,2},{12,4},{14,6},{1,9},{3,11}... | collective-permute-start | bytes 393224 | tf_op jit(solution)/shard_map/ppermute | solution.py:13
  32.3 6.2 %collective-permute-start.3 = (f32[64,512]{1,0:T(8,128)S(1)}, f32[64,512]{1,0:T(8,128)S(1)}, u32[]{:S(2)}, u32[]{:S(2)}) collective-permute-start(f32[64,512]{1,0:T(8,128)S(1)} %maximum_select_fusion), channel_id=1, source_target_pairs={{0,16},{1,17},{2,18},{3,19},{4,20},{5,21},{6,22},{7,23},{8,24},{9,... | collective-permute-start | bytes 393224 | tf_op jit(solution)/shard_map/ppermute | solution.py:22
  45.2 5.0 %collective-permute-start.4 = (f32[64,512]{1,0:T(8,128)S(1)}, f32[64,512]{1,0:T(8,128)S(1)}, u32[]{:S(2)}, u32[]{:S(2)}) collective-permute-start(f32[64,512]{1,0:T(8,128)S(1)} %fusion.8), channel_id=1, source_target_pairs={{0,2},{2,0},{4,6},{6,4},{8,10},{10,8},{12,14},{14,12},{1,3},{3,1},... | collective-permute-start | bytes 393224 | tf_op jit(solution)/shard_map/ppermute | solution.py:13
  50.2 5.5 %collective-permute-start.5 = (f32[64,512]{1,0:T(8,128)S(1)}, f32[64,512]{1,0:T(8,128)S(1)}, u32[]{:S(2)}, u32[]{:S(2)}) collective-permute-start(f32[64,512]{1,0:T(8,128)S(1)} %add.181), channel_id=1, source_target_pairs={{0,4},{2,6},{4,0},{6,2},{8,12},{10,14},{12,8},{14,10},{1,5},{3,7},... | collective-permute-start | bytes 393224 | tf_op jit(solution)/shard_map/ppermute | solution.py:13
  55.7 7.3 %collective-permute-start.6 = (f32[64,512]{1,0:T(8,128)S(1)}, f32[64,512]{1,0:T(8,128)S(1)}, u32[]{:S(2)}, u32[]{:S(2)}) collective-permute-start(f32[64,512]{1,0:T(8,128)S(1)} %add.182), channel_id=1, source_target_pairs={{0,8},{2,10},{4,12},{6,14},{8,0},{10,2},{12,4},{14,6},{1,9},{3,11}... | collective-permute-start | bytes 393224 | tf_op jit(solution)/shard_map/ppermute | solution.py:13
  63.2 6.9 %collective-permute-start.7 = (f32[64,512]{1,0:T(8,128)S(1)}, f32[64,512]{1,0:T(8,128)}, u32[]{:S(2)}, u32[]{:S(2)}) collective-permute-start(f32[64,512]{1,0:T(8,128)S(1)} %maximum_select_fusion.2), channel_id=1, source_target_pairs={{0,16},{1,17},{2,18},{3,19},{4,20},{5,21},{6,22},{7,23},{8,24},{9,... | collective-permute-start | bytes 393224 | tf_op jit(solution)/shard_map/ppermute | solution.py:22
  77.5 5.0 %collective-permute-start.8 = (f32[64,512]{1,0:T(8,128)S(1)}, f32[64,512]{1,0:T(8,128)S(1)}, u32[]{:S(2)}, u32[]{:S(2)}) collective-permute-start(f32[64,512]{1,0:T(8,128)S(1)} %fusion.7), channel_id=1, source_target_pairs={{0,2},{2,0},{4,6},{6,4},{8,10},{10,8},{12,14},{14,12},{1,3},{3,1},... | collective-permute-start | bytes 393224 | tf_op jit(solution)/shard_map/ppermute | solution.py:13
  82.6 5.0 %collective-permute-start.9 = (f32[64,512]{1,0:T(8,128)S(1)}, f32[64,512]{1,0:T(8,128)S(1)}, u32[]{:S(2)}, u32[]{:S(2)}) collective-permute-start(f32[64,512]{1,0:T(8,128)S(1)} %add.189), channel_id=1, source_target_pairs={{0,4},{2,6},{4,0},{6,2},{8,12},{10,14},{12,8},{14,10},{1,5},{3,7},... | collective-permute-start | bytes 393224 | tf_op jit(solution)/shard_map/ppermute | solution.py:13
  87.7 7.3 %collective-permute-start.10 = (f32[64,512]{1,0:T(8,128)S(1)}, f32[64,512]{1,0:T(8,128)S(1)}, u32[]{:S(2)}, u32[]{:S(2)}) collective-permute-start(f32[64,512]{1,0:T(8,128)S(1)} %add.190), channel_id=1, source_target_pairs={{0,8},{2,10},{4,12},{6,14},{8,0},{10,2},{12,4},{14,6},{1,9},{3,11}... | collective-permute-start | bytes 393224 | tf_op jit(solution)/shard_map/ppermute | solution.py:13
  95.1 7.0 %collective-permute-start.11 = (f32[64,512]{1,0:T(8,128)S(1)}, f32[64,512]{1,0:T(8,128)}, u32[]{:S(2)}, u32[]{:S(2)}) collective-permute-start(f32[64,512]{1,0:T(8,128)S(1)} %maximum_select_fusion.4), channel_id=1, source_target_pairs={{0,16},{1,17},{2,18},{3,19},{4,20},{5,21},{6,22},{7,23},{8,24},{9,... | collective-permute-start | bytes 393224 | tf_op jit(solution)/shard_map/ppermute | solution.py:22
  109.6 5.0 %collective-permute-start.12 = (f32[64,512]{1,0:T(8,128)S(1)}, f32[64,512]{1,0:T(8,128)S(1)}, u32[]{:S(2)}, u32[]{:S(2)}) collective-permute-start(f32[64,512]{1,0:T(8,128)S(1)} %fusion.6), channel_id=1, source_target_pairs={{0,2},{2,0},{4,6},{6,4},{8,10},{10,8},{12,14},{14,12},{1,3},{3,1},... | collective-permute-start | bytes 393224 | tf_op jit(solution)/shard_map/ppermute | solution.py:13
  114.6 5.0 %collective-permute-start.13 = (f32[64,512]{1,0:T(8,128)S(1)}, f32[64,512]{1,0:T(8,128)S(1)}, u32[]{:S(2)}, u32[]{:S(2)}) collective-permute-start(f32[64,512]{1,0:T(8,128)S(1)} %add.197), channel_id=1, source_target_pairs={{0,4},{2,6},{4,0},{6,2},{8,12},{10,14},{12,8},{14,10},{1,5},{3,7},... | collective-permute-start | bytes 393224 | tf_op jit(solution)/shard_map/ppermute | solution.py:13
  119.7 6.8 %collective-permute-start.14 = (f32[64,512]{1,0:T(8,128)S(1)}, f32[64,512]{1,0:T(8,128)S(1)}, u32[]{:S(2)}, u32[]{:S(2)}) collective-permute-start(f32[64,512]{1,0:T(8,128)S(1)} %add.198), channel_id=1, source_target_pairs={{0,8},{2,10},{4,12},{6,14},{8,0},{10,2},{12,4},{14,6},{1,9},{3,11}... | collective-permute-start | bytes 393224 | tf_op jit(solution)/shard_map/ppermute | solution.py:13
  126.6 7.0 %collective-permute-start.15 = (f32[64,512]{1,0:T(8,128)S(1)}, f32[64,512]{1,0:T(8,128)S(1)}, u32[]{:S(2)}, u32[]{:S(2)}) collective-permute-start(f32[64,512]{1,0:T(8,128)S(1)} %maximum_select_fusion.6), channel_id=1, source_target_pairs={{0,16},{1,17},{2,18},{3,19},{4,20},{5,21},{6,22},{7,23},{8,24},{9,... | collective-permute-start | bytes 393224 | tf_op jit(solution)/shard_map/ppermute | solution.py:22
  140.2 5.0 %collective-permute-start.16 = (f32[64,512]{1,0:T(8,128)S(1)}, f32[64,512]{1,0:T(8,128)S(1)}, u32[]{:S(2)}, u32[]{:S(2)}) collective-permute-start(f32[64,512]{1,0:T(8,128)S(1)} %fusion.5), channel_id=1, source_target_pairs={{0,2},{2,0},{4,6},{6,4},{8,10},{10,8},{12,14},{14,12},{1,3},{3,1},... | collective-permute-start | bytes 393224 | tf_op jit(solution)/shard_map/ppermute | solution.py:13
  145.3 5.0 %collective-permute-start.17 = (f32[64,512]{1,0:T(8,128)S(1)}, f32[64,512]{1,0:T(8,128)S(1)}, u32[]{:S(2)}, u32[]{:S(2)}) collective-permute-start(f32[64,512]{1,0:T(8,128)S(1)} %add.205), channel_id=1, source_target_pairs={{0,4},{2,6},{4,0},{6,2},{8,12},{10,14},{12,8},{14,10},{1,5},{3,7},... | collective-permute-start | bytes 393224 | tf_op jit(solution)/shard_map/ppermute | solution.py:13
  150.3 6.8 %collective-permute-start.18 = (f32[64,512]{1,0:T(8,128)S(1)}, f32[64,512]{1,0:T(8,128)S(1)}, u32[]{:S(2)}, u32[]{:S(2)}) collective-permute-start(f32[64,512]{1,0:T(8,128)S(1)} %add.206), channel_id=1, source_target_pairs={{0,8},{2,10},{4,12},{6,14},{8,0},{10,2},{12,4},{14,6},{1,9},{3,11}... | collective-permute-start | bytes 393224 | tf_op jit(solution)/shard_map/ppermute | solution.py:13
